TPU v7x, 32 devices: a whole 2x2x4 slice. The times are simulated.
32 devices in a mesh: dp: 16 (over z, y, x), mp: 2 (over core).
Axes of the slice: x: 2, y: 2, z: 4, core: 2. Of those that a mesh axis runs over, the one named last changes fastest.
Arguments:
- value_grads: bfloat16 [16, 24, 128, 128], P('dp', 'mp'), may hold values from -2 to 2
- key_grads: bfloat16 [16, 2, 16, 128, 128], P('dp', 'mp'), may hold values from -0.75 to 0.75
- owners: int32 [40, 1], P('mp'), may hold values from 0 to 15; in each aligned block of 20 rows (0 to 19, 20 to 39, ...) at most 2 rows name the same one
- weights: float32 [16, 2, 2, 128, 128], P('dp', 'mp'), may hold values from -6 to 6
- left: float32 [16, 2, 2, 128, 128], P('dp', 'mp'), may hold values from -0.25 to 4, as said below
- right: float32 [16, 2, 2, 128, 128], P('dp', 'mp'), may hold values from -0.25 to 4, as said below
- left_root: float32 [16, 2, 2, 128, 128], P('dp', 'mp'), may hold values from -0.25 to 4
- right_root: float32 [16, 2, 2, 128, 128], P('dp', 'mp'), may hold values from -0.25 to 4
- second: float32 [16, 2, 2, 128, 128], P('dp', 'mp'), may hold values from 0.001 to 0.1
Outputs:
- new_weights: float32 [16, 2, 2, 128, 128], P('dp', 'mp')
- new_left: float32 [16, 2, 2, 128, 128], P('dp', 'mp')
- new_right: float32 [16, 2, 2, 128, 128], P('dp', 'mp')
- new_second: float32 [16, 2, 2, 128, 128], P('dp', 'mp')
- new_values: bfloat16 [24, 128, 128], P('mp')
- new_keys: bfloat16 [16, 128, 128], P('mp')
Inputs may be any that keep to these rules, and one draw needn't show every extreme that they name: `owners`: within each aligned block of 20 rows (one index of mp) no dp index appears more than 2 times; some appears exactly 2 times. `left`: Symmetric. `right`: Symmetric.
All inputs are finite; a program needn't handle non-finite values.
Results may differ from a plain program's by a relative error of at most 0.0035.
Values may be sent and summed in bfloat16 or wider, within the bound.
A program may use at most 64 MiB of HBM per device.

v0:
```python
import jax
import jax.numpy as jnp
from jax import lax
from jax.sharding import PartitionSpec as P

STAT_DECAY = 0.95
ADAM_DECAY = 0.95
LEARN_RATE = 0.1
NORM_EPS = 1e-06


def slot_onehot(owner_ids, capacity, slot_count):
    position = jnp.arange(owner_ids.shape[0], dtype=jnp.int32)
    same_owner = owner_ids[:, None] == owner_ids[None, :]
    earlier = position[None, :] < position[:, None]
    slot_rank = jnp.sum((same_owner & earlier).astype(jnp.int32), axis=1)
    target = owner_ids * capacity + slot_rank
    return (target[:, None] == jnp.arange(slot_count, dtype=jnp.int32)[None, :]).astype(
        jnp.bfloat16
    )


def shampoo(gradient, weights, left, right, left_root, right_root, second):
    high = lax.Precision.HIGHEST
    new_left = STAT_DECAY * left + (1.0 - STAT_DECAY) * jnp.einsum(
        "...ij,...kj->...ik", gradient, gradient, precision=high
    )
    new_right = STAT_DECAY * right + (1.0 - STAT_DECAY) * jnp.einsum(
        "...ji,...jk->...ik", gradient, gradient, precision=high
    )
    shaped = jnp.einsum("...ij,...jk->...ik", left_root, gradient, precision=high)
    shaped = jnp.einsum("...ij,...jk->...ik", shaped, right_root, precision=high)
    new_second = ADAM_DECAY * second + (1.0 - ADAM_DECAY) * gradient * gradient
    adam_step = gradient / jnp.sqrt(new_second)
    adam_norm = jnp.sqrt(jnp.sum(adam_step * adam_step, axis=(-2, -1), keepdims=True))
    shaped_norm = jnp.sqrt(jnp.sum(shaped * shaped, axis=(-2, -1), keepdims=True))
    graft_scale = adam_norm / (shaped_norm + NORM_EPS)
    new_weights = weights - LEARN_RATE * graft_scale * shaped
    return (new_weights, new_left, new_right, new_second)


def on_device(value_grads, key_grads, owners, weights, left, right, left_root, right_root, second):
    dp_count = lax.axis_size("dp")
    capacity = weights.shape[2]
    slot_count = dp_count * capacity
    value_count = value_grads.shape[1]
    side = value_grads.shape[2]
    key_part = lax.psum_scatter(
        key_grads.astype(jnp.float32).astype(jnp.bfloat16), "mp", scatter_dimension=2, tiled=True
    ).astype(jnp.float32)
    key_rows = key_part[0, 0].astype(jnp.bfloat16)
    one_hot = slot_onehot(owners[:, 0], capacity, slot_count)
    blocks = jnp.concatenate([value_grads[0], key_rows], axis=0)
    placed = jnp.einsum("bj,bxy->jxy", one_hot, blocks, preferred_element_type=jnp.float32)
    outgoing = placed.astype(jnp.bfloat16).reshape(dp_count, capacity, side, side)
    incoming = lax.all_to_all(outgoing, "dp", split_axis=0, concat_axis=0, tiled=True)
    gradient = jnp.sum(incoming, axis=0, dtype=jnp.float32)
    new_weights, new_left, new_right, new_second = shampoo(
        gradient,
        weights[0, 0],
        left[0, 0],
        right[0, 0],
        left_root[0, 0],
        right_root[0, 0],
        second[0, 0],
    )
    rounded = new_weights.astype(jnp.bfloat16)
    everyone = lax.all_gather(rounded, "dp", axis=0, tiled=True)
    picked = jnp.einsum(
        "bj,jxy->bxy", one_hot, everyone, preferred_element_type=jnp.float32
    ).astype(jnp.bfloat16)
    return (
        new_weights[None, None],
        new_left[None, None],
        new_right[None, None],
        new_second[None, None],
        picked[:value_count],
        picked[value_count:],
    )


def solution(mesh):
    return jax.shard_map(
        on_device,
        mesh=mesh,
        in_specs=(
            P("dp", "mp", None, None),
            P("dp", "mp", None, None, None),
            P("mp", None),
            P("dp", "mp", None, None, None),
            P("dp", "mp", None, None, None),
            P("dp", "mp", None, None, None),
            P("dp", "mp", None, None, None),
            P("dp", "mp", None, None, None),
            P("dp", "mp", None, None, None),
        ),
        out_specs=(
            P("dp", "mp", None, None, None),
            P("dp", "mp", None, None, None),
            P("dp", "mp", None, None, None),
            P("dp", "mp", None, None, None),
            P("mp", None, None),
            P("mp", None, None),
        ),
        check_vma=False,
    )
```

profile of v0, /device:TPU:0, one launch (start us, length us, event | category | flops | bytes accessed | tf_op | source)
XLA Modules:
  0.0 123.6 jit_solution(12774246260677728813)
XLA Ops:
  7.2 0.0 copy-start
  7.2 0.0 copy-start.2
  7.2 0.0 reduce-scatter.4.cloned.1.call-start
  7.2 0.0 copy-start.7
  7.2 2.2 %copy.86 = bf16[2,8,128,128]{3,1,2,0:T(8,128)(2,1)} copy(bf16[2,8,128,128]{3,2,1,0:T(8,128)(2,1)} %bitcast.74) | data formatting | bytes 1048576
  9.5 0.0 reduce-scatter.4.cloned.1.call-update
  9.5 0.0 all-gather.2.cloned.1.call-start
  9.5 0.0 copy-done.2
  9.6 0.3 copy.87
  9.8 0.0 copy-done.7
  9.8 0.2 convert_reduce_fusion.1
  10.0 10.9 %reduce-scatter.4.cloned.1.call-done = bf16[8,16384]{1,0:T(8,128)(2,1)} async-done(((bf16[16,16384]{1,0:T(8,128)(2,1)}), bf16[8,16384]{1,0:T(8,128)(2,1)}) %reduce-scatter.4.cloned.1.call-update) | async-done | bytes 262160
  20.9 1.0 copy.88
  21.9 0.2 copy.89
  22.1 0.6 convolution_convert_fusion
  22.7 1.0 copy.55
  23.6 33.3 %all_to_all.5 = bf16[16,2,128,128]{3,1,2,0:T(2,128)(2,1)S(1)} all-to-all(bf16[16,2,128,128]{3,1,2,0:T(2,128)(2,1)S(1)} %copy.55), channel_id=1, replica_groups=mesh['dp'=16,'mp'=2] {'dp'}, dimensions={0} | all-to-all | bytes 2097152 | tf_op jit(solution)/shard_map/all_to_all | solution.py:56
  56.9 0.1 convert_reduce_fusion
  57.0 0.8 copy-done.3
  57.8 0.3 fusion.16
  58.1 0.1 fusion.12
  58.2 0.4 multiply_reduce_fusion
  58.6 0.8 fusion.18
  59.4 0.0 all-gather.2.cloned.1.call-update
  59.4 1.0 fusion.1
  60.5 1.0 fusion.3
  61.5 0.7 fusion.13
  62.2 50.9 %all-gather.2.cloned.1.call-done = bf16[32,128,128]{2,1,0:T(8,128)(2,1)} async-done(((bf16[2,128,128]{2,1,0:T(8,128)(2,1)}), bf16[32,128,128]{2,1,0:T(8,128)(2,1)}) %all-gather.2.cloned.1.call-update) | async-done | bytes 1048592 | tf_op jit(solution)/shard_map/all_gather | solution.py:68
  113.1 2.0 %convolution_convert_fusion.1 = bf16[20,128,128]{2,0,1:T(8,128)(2,1)S(1)} fusion(bf16[32,128,128]{2,1,0:T(8,128)(2,1)} %all-gather.2.cloned.1.call-done, s32[20]{0:T(128)S(1)} %fusion.26), kind=kOutput, calls=%fused_computation.2 | convolution fusion | flops 21299840 | bytes 1704016 | tf_op jit(solution)/shard_map/bj,jxy->bxy/dot_general | solution.py:69
  115.1 0.1 slice.9
  115.2 0.8 copy.69
  116.0 0.7 copy.70
  (13 shorter events, 0.1 us)
Async XLA Ops:
  7.2 51.0 %copy-start = (f32[1,1,2,128,128]{4,3,2,1,0:T(8,128)S(1)}, f32[1,1,2,128,128]{4,3,2,1,0:T(8,128)}, u32[]{:S(2)}) copy-start(f32[1,1,2,128,128]{4,3,2,1,0:T(8,128)} %param.16) | copy-start | bytes 393220
  7.2 2.4 %copy-start.2 = (bf16[1,12,128,128]{3,2,1,0:T(8,128)(2,1)S(1)}, bf16[1,12,128,128]{3,2,1,0:T(8,128)(2,1)}, u32[]{:S(2)}) copy-start(bf16[1,12,128,128]{3,2,1,0:T(8,128)(2,1)} %param.9) | copy-start | bytes 1179652
  7.2 13.7 %reduce-scatter.4.cloned.1.call-start = ((), (), s32[]{:S(2)}) async-start(), calls=%async_computation.3 | async-start | bytes 786432
  7.2 2.6 %copy-start.7 = (s32[20,1]{0,1:T(1,128)S(1)}, s32[20,1]{0,1:T(1,128)}, u32[]{:S(2)}) copy-start(s32[20,1]{0,1:T(1,128)} %param.11) | copy-start | bytes 244
  9.5 103.6 %all-gather.2.cloned.1.call-start = ((), (), s32[]{:S(2)}) async-start(), calls=%async_computation.2 | async-start | bytes 1114112 | tf_op jit(solution)/shard_map/all_gather | solution.py:68
  56.9 0.9 copy-start.3
  56.9 1.2 copy-start.1
  56.9 1.7 %copy-start.4 = (f32[1,1,2,128,128]{4,3,2,1,0:T(8,128)S(1)}, f32[1,1,2,128,128]{4,3,2,1,0:T(8,128)}, u32[]{:S(2)}) copy-start(f32[1,1,2,128,128]{4,3,2,1,0:T(8,128)} %param.12) | copy-start | bytes 393220
  57.8 1.6 %copy-start.5 = (f32[1,1,2,128,128]{4,3,2,1,0:T(8,128)S(1)}, f32[1,1,2,128,128]{4,3,2,1,0:T(8,128)}, u32[]{:S(2)}) copy-start(f32[1,1,2,128,128]{4,3,2,1,0:T(8,128)} %param.14) | copy-start | bytes 393220
  57.8 2.7 %copy-start.6 = (f32[1,1,2,128,128]{4,3,2,1,0:T(8,128)S(1)}, f32[1,1,2,128,128]{4,3,2,1,0:T(8,128)}, u32[]{:S(2)}) copy-start(f32[1,1,2,128,128]{4,3,2,1,0:T(8,128)} %param.13) | copy-start | bytes 393220
Sparse Core Ops, SparseCore 0:
  10.2 10.6 reduce-scatter.3
  59.5 53.5 all-gather.1
where the time goes:
time: 124 us
  waiting for transfers between devices  61.8 us (50%)
  blocking collectives  33.3 us (27%)
  between operations  14.2 us (11%)
  local copies, waits for them, and re-layouts  7.18 us (6%)
  matrix products  5.23 us (4%)
  other arithmetic  1.86 us (2%)
    all_gather x1, waiting for transfers between devices, on_device(): everyone = lax.all_gather(rounded, 'dp', axis=0, tiled=True)  50.9 us
    all_to_all x1, blocking collectives, on_device(): lax.all_to_all(outgoing, 'dp', split_axis=0, concat_axis=0, tiled=True)  33.3 us
    unnamed x3, waiting for transfers between devices  10.9 us
    unnamed x22, local copies, waits for them, and re-layouts  6.1 us
  transfers between devices with their start and end apart: 2, of which 2 were waited for; matrix products, arithmetic and copies ran while one was open for 3% of the time, Pallas kernels for 0%

commit v1 on v0

--- a/solution.py
+++ b/solution.py
@@ -1,3 +1,4 @@
+import functools
 import jax
 import jax.numpy as jnp
 from jax import lax
@@ -7,6 +8,30 @@
 ADAM_DECAY = 0.95
 LEARN_RATE = 0.1
 NORM_EPS = 1e-06
+
+
+def lead_edge_for(xs, axis_no):
+    val, block_now, taken_in = (
+        jax.lax.axis_size("dp"),
+        jax.lax.axis_index("dp"),
+        xs.shape[axis_no],
+    )
+    all_values, outcome_arr = (xs, 1)
+    while outcome_arr < val:
+        all_values = jnp.concatenate(
+            [
+                all_values,
+                jax.lax.ppermute(
+                    all_values, "dp", tuple(((at, (at - outcome_arr) % val) for at in range(val)))
+                ),
+            ],
+            axis_no,
+        )
+        outcome_arr = 2 * outcome_arr
+    return jnp.roll(all_values, block_now * taken_in, axis_no)
+
+
+_convert_links = functools.partial(lead_edge_for, axis_no=0)
 
 
 def slot_onehot(owner_ids, capacity, slot_count):
@@ -65,7 +90,7 @@
         second[0, 0],
     )
     rounded = new_weights.astype(jnp.bfloat16)
-    everyone = lax.all_gather(rounded, "dp", axis=0, tiled=True)
+    everyone = _convert_links(rounded)
     picked = jnp.einsum(
         "bj,jxy->bxy", one_hot, everyone, preferred_element_type=jnp.float32
     ).astype(jnp.bfloat16)

time: 124 us -> 110 us (0.89)
  the two profiles are of different devices: /device:TPU:0 before, /device:TPU:31 now
where the time goes in v1:
time: 110 us
  waiting for transfers between devices  51.2 us (47%)
  blocking collectives  29.5 us (27%)
  between operations  14.3 us (13%)
  local copies, waits for them, and re-layouts  7.72 us (7%)
  matrix products  4.02 us (4%)
  other arithmetic  2.01 us (2%)
  starting transfers between devices  1.37 us (1%)
    ppermute x4, waiting for transfers between devices, lead_edge_for(): jax.lax.ppermute(all_values, 'dp', tuple(((at, (at - outcome_arr) % val)...  42.2 us
    all_to_all x1, blocking collectives, on_device(): lax.all_to_all(outgoing, 'dp', split_axis=0, concat_axis=0, tiled=True)  29.5 us
    unnamed x2, waiting for transfers between devices  8.94 us
    unnamed x28, local copies, waits for them, and re-layouts  6.46 us
  transfers between devices with their start and end apart: 5, of which 5 were waited for; matrix products, arithmetic and copies ran while one was open for 5% of the time, Pallas kernels for 0%

profile of v1, /device:TPU:31, one launch (start us, length us, event | category | flops | bytes accessed | tf_op | source)
XLA Modules:
  0.0 110.0 jit_solution(12268200680307725274)
XLA Ops:
  7.2 2.2 %copy.86 = bf16[2,8,128,128]{3,1,2,0:T(8,128)(2,1)} copy(bf16[2,8,128,128]{3,2,1,0:T(8,128)(2,1)} %bitcast.75) | data formatting | bytes 1048576
  9.4 1.3 %copy.87 = bf16[1,12,128,128]{3,1,2,0:T(8,128)(2,1)S(1)} copy(bf16[1,12,128,128]{3,2,1,0:T(8,128)(2,1)} %param.9) | data formatting | bytes 786432 | tf_op args[0]
  10.7 0.2 convert_reduce_fusion.1
  10.9 8.9 %reduce-scatter.4.cloned.1.call-done = bf16[8,16384]{1,0:T(8,128)(2,1)} async-done(((bf16[16,16384]{1,0:T(8,128)(2,1)}), bf16[8,16384]{1,0:T(8,128)(2,1)}) %reduce-scatter.4.cloned.1.call-update) | async-done | bytes 262160
  19.8 1.0 copy.88
  20.8 0.2 copy.89
  21.0 0.6 convolution_convert_fusion
  21.6 1.0 copy.55
  22.6 29.5 %all_to_all.5 = bf16[16,2,128,128]{3,1,2,0:T(2,128)(2,1)S(1)} all-to-all(bf16[16,2,128,128]{3,1,2,0:T(2,128)(2,1)S(1)} %copy.55), channel_id=1, replica_groups=mesh['dp'=16,'mp'=2] {'dp'}, dimensions={0} | all-to-all | bytes 2097152 | tf_op jit(solution)/shard_map/all_to_all | solution.py:81
  52.0 0.1 convert_reduce_fusion
  52.1 0.3 fusion.16
  52.4 0.1 fusion.12
  52.6 0.4 multiply_reduce_fusion
  53.0 0.1 constant_dynamic-update-slice_fusion.9
  53.1 1.1 %collective-permute-start = (bf16[2,128,128]{2,1,0:T(8,128)(2,1)S(1)}, bf16[2,128,128]{2,1,0:T(8,128)(2,1)S(1)}, u32[]{:S(2)}, u32[]{:S(2)}) collective-permute-start(bf16[2,128,128]{2,1,0:T(8,128)(2,1)S(1)} %get-tuple-element.31), channel_id=1, source_target_pairs={{0,30},{2,0},{4,2},{6,4},{8,6},{10,8},{12,10},{14,12},{16,14},{18,... | collective-permute-start | bytes 196616 | tf_op jit(solution)/shard_map/ppermute | solution.py:24
  54.2 5.6 %collective-permute-done = bf16[2,128,128]{2,1,0:T(8,128)(2,1)S(1)} collective-permute-done((bf16[2,128,128]{2,1,0:T(8,128)(2,1)S(1)}, bf16[2,128,128]{2,1,0:T(8,128)(2,1)S(1)}, u32[]{:S(2)}, u32[]{:S(2)}) %collective-permute-start) | collective-permute-done | bytes 65568 | tf_op jit(solution)/shard_map/ppermute | solution.py:24
  59.8 0.1 collective-permute-start.1
  59.9 6.5 %collective-permute-done.1 = bf16[4,128,128]{2,1,0:T(8,128)(2,1)S(1)} collective-permute-done((bf16[4,128,128]{2,1,0:T(8,128)(2,1)S(1)}, bf16[4,128,128]{2,1,0:T(8,128)(2,1)S(1)}, u32[]{:S(2)}, u32[]{:S(2)}) %collective-permute-start.1) | collective-permute-done | bytes 131104 | tf_op jit(solution)/shard_map/ppermute | solution.py:24
  66.5 0.7 fusion.13
  67.2 0.7 fusion.19
  67.9 5.6 %collective-permute-done.2 = bf16[8,128,128]{2,1,0:T(8,128)(2,1)S(1)} collective-permute-done((bf16[8,128,128]{2,1,0:T(8,128)(2,1)S(1)}, bf16[8,128,128]{2,1,0:T(8,128)(2,1)S(1)}, u32[]{:S(2)}, u32[]{:S(2)}) %collective-permute-start.2) | collective-permute-done | bytes 262176 | tf_op jit(solution)/shard_map/ppermute | solution.py:24
  73.6 0.1 collective-permute-start.3
  73.7 1.0 fusion.1
  74.7 1.0 fusion.3
  75.8 24.5 %collective-permute-done.3 = bf16[16,128,128]{2,1,0:T(8,128)(2,1)S(1)} collective-permute-done((bf16[16,128,128]{2,1,0:T(8,128)(2,1)S(1)}, bf16[16,128,128]{2,1,0:T(8,128)(2,1)S(1)}, u32[]{:S(2)}, u32[]{:S(2)}) %collective-permute-start.3) | collective-permute-done | bytes 524320 | tf_op jit(solution)/shard_map/ppermute | solution.py:24
  100.4 0.1 constant_dynamic-update-slice_fusion.5
  100.5 0.1 constant_dynamic-update-slice_fusion
  100.6 0.1 constant_dynamic-slice_fusion
  100.7 0.7 convolution_convert_fusion.1
  101.5 0.1 slice.9
  101.6 0.8 copy.69
  102.5 0.7 copy.70
  (30 shorter events, 0.5 us)
Async XLA Ops:
  7.2 45.4 %copy-start = (f32[1,1,2,128,128]{4,3,2,1,0:T(8,128)S(1)}, f32[1,1,2,128,128]{4,3,2,1,0:T(8,128)}, u32[]{:S(2)}) copy-start(f32[1,1,2,128,128]{4,3,2,1,0:T(8,128)} %param.16) | copy-start | bytes 393220
  7.2 3.5 %copy-start.6 = (s32[20,1]{0,1:T(1,128)S(1)}, s32[20,1]{0,1:T(1,128)}, u32[]{:S(2)}) copy-start(s32[20,1]{0,1:T(1,128)} %param.11) | copy-start | bytes 244
  7.2 12.6 %reduce-scatter.4.cloned.1.call-start = ((), (), s32[]{:S(2)}) async-start(), calls=%async_computation.2 | async-start | bytes 786432
  22.5 29.6 %copy-start.3 = (f32[1,1,2,128,128]{4,3,2,1,0:T(8,128)S(1)}, f32[1,1,2,128,128]{4,3,2,1,0:T(8,128)}, u32[]{:S(2)}) copy-start(f32[1,1,2,128,128]{4,3,2,1,0:T(8,128)} %param.15) | copy-start | bytes 393220
  22.5 29.9 %copy-start.1 = (f32[1,1,2,128,128]{4,3,2,1,0:T(8,128)S(1)}, f32[1,1,2,128,128]{4,3,2,1,0:T(8,128)}, u32[]{:S(2)}) copy-start(f32[1,1,2,128,128]{4,3,2,1,0:T(8,128)} %param.17) | copy-start | bytes 393220
  22.6 30.4 %copy-start.2 = (f32[1,1,2,128,128]{4,3,2,1,0:T(8,128)S(1)}, f32[1,1,2,128,128]{4,3,2,1,0:T(8,128)}, u32[]{:S(2)}) copy-start(f32[1,1,2,128,128]{4,3,2,1,0:T(8,128)} %param.12) | copy-start | bytes 393220
  52.1 21.5 %copy-start.4 = (f32[1,1,2,128,128]{4,3,2,1,0:T(8,128)S(1)}, f32[1,1,2,128,128]{4,3,2,1,0:T(8,128)}, u32[]{:S(2)}) copy-start(f32[1,1,2,128,128]{4,3,2,1,0:T(8,128)} %param.14) | copy-start | bytes 393220
  52.4 22.3 %copy-start.5 = (f32[1,1,2,128,128]{4,3,2,1,0:T(8,128)S(1)}, f32[1,1,2,128,128]{4,3,2,1,0:T(8,128)}, u32[]{:S(2)}) copy-start(f32[1,1,2,128,128]{4,3,2,1,0:T(8,128)} %param.13) | copy-start | bytes 393220
  53.1 6.8 %collective-permute-start = (bf16[2,128,128]{2,1,0:T(8,128)(2,1)S(1)}, bf16[2,128,128]{2,1,0:T(8,128)(2,1)S(1)}, u32[]{:S(2)}, u32[]{:S(2)}) collective-permute-start(bf16[2,128,128]{2,1,0:T(8,128)(2,1)S(1)} %get-tuple-element.31), channel_id=1, source_target_pairs={{0,30},{2,0},{4,2},{6,4},{8,6},{10,8},{12,10},{14,12},{16,14},{18,... | collective-permute-start | bytes 196616 | tf_op jit(solution)/shard_map/ppermute | solution.py:24
  59.8 6.6 %collective-permute-start.1 = (bf16[4,128,128]{2,1,0:T(8,128)(2,1)S(1)}, bf16[4,128,128]{2,1,0:T(8,128)(2,1)S(1)}, u32[]{:S(2)}, u32[]{:S(2)}) collective-permute-start(bf16[4,128,128]{2,1,0:T(8,128)(2,1)S(1)} %pad_maximum_fusion.2), channel_id=1, source_target_pairs={{0,28},{2,30},{4,0},{6,2},{8,4},{10,6},{12,8},{14,10},{16,12},{18,... | collective-permute-start | bytes 393224 | tf_op jit(solution)/shard_map/ppermute | solution.py:24
  66.4 7.1 %collective-permute-start.2 = (bf16[8,128,128]{2,1,0:T(8,128)(2,1)S(1)}, bf16[8,128,128]{2,1,0:T(8,128)(2,1)S(1)}, u32[]{:S(2)}, u32[]{:S(2)}) collective-permute-start(bf16[8,128,128]{2,1,0:T(8,128)(2,1)S(1)} %pad_maximum_fusion.1), channel_id=1, source_target_pairs={{0,24},{2,26},{4,28},{6,30},{8,0},{10,2},{12,4},{14,6},{16,8},{18,... | collective-permute-start | bytes 786440 | tf_op jit(solution)/shard_map/ppermute | solution.py:24
  73.6 26.8 %collective-permute-start.3 = (bf16[16,128,128]{2,1,0:T(8,128)(2,1)S(1)}, bf16[16,128,128]{2,1,0:T(8,128)(2,1)S(1)}, u32[]{:S(2)}, u32[]{:S(2)}) collective-permute-start(bf16[16,128,128]{2,1,0:T(8,128)(2,1)S(1)} %pad_maximum_fusion), channel_id=1, source_target_pairs={{0,16},{2,18},{4,20},{6,22},{8,24},{10,26},{12,28},{14,30},{16,0},... | collective-permute-start | bytes 1572872 | tf_op jit(solution)/shard_map/ppermute | solution.py:24
Sparse Core Ops, SparseCore 0:
  10.2 9.5 reduce-scatter.3
